TPU v7x, 128 devices: a whole 4x4x4 slice. The times are simulated.
128 devices in a mesh: wide: 16 (over y, z), narrow: 8 (over x, core).
Axes of the slice: x: 4, y: 4, z: 4, core: 2. Of those that a mesh axis runs over, the one named last changes fastest.
Arguments:
- hidden: bfloat16 [128, 16384], P('narrow', 'wide'), may hold values from -6 to 6
- gain: bfloat16 [16384], P('wide'), may hold values from 0.5 to 1.5
- sign_in: int32 [16384], P('wide'), may hold values from 0 to 1
- qkv_weight: bfloat16 [16384, 18432], P('wide', 'narrow'), may hold values from -0.046875 to 0.046875
- out_weight: bfloat16 [16384, 16384], P('narrow', 'wide'), may hold values from -0.046875 to 0.046875
- sign_attn: int32 [16384], P('narrow'), may hold values from 0 to 1
- key_cache: bfloat16 [128, 8, 4096, 128], P('wide', 'narrow'), may hold values from -512 to 512, as said below
- value_cache: bfloat16 [128, 8, 4096, 128], P('wide', 'narrow'), may hold values from -6 to 6
- lengths: int32 [128], P('wide'), may hold values from 1024 to 4096
Outputs:
- layer_out: bfloat16 [128, 16384], P('narrow', 'wide')
Inputs may be any that keep to these rules, and one draw needn't show every extreme that they name: `key_cache`: cached keys mostly of magnitude about 2, with some slots far larger in the hidden draw.
All inputs are finite; a program needn't handle non-finite values. Where the computation divides by a largest or mean magnitude, that divisor is 1e-20 or more.
Results may differ from a plain program's by a relative error of at most 0.018.
Values may be sent and summed in bfloat16 or wider, within the bound.
No kernel may reach another device: no remote copies, remote signals or barrier semaphores. Data moves between devices by JAX's collectives and lax.ppermute only.
A program may use at most 128 MiB of HBM per device.

v0:
```python
import math
import jax
import jax.numpy as jnp
from jax import lax
from jax.sharding import Mesh
from jax.sharding import PartitionSpec as P

D = 16384
HD = 128
QG = 16
WIDE = ("wide_0", "wide_1")
ROPE_BASE = 500000.0


def one_axis_at_a_time(value, axes):
    for axis in axes:
        value = lax.psum(value, axis)
    return value


def side_by_side(arrays, axis, dim, along):
    columns = [a.reshape(*a.shape[:along], -1) for a in arrays]
    both = jnp.concatenate(columns, axis=along)
    filled, at, gathered = (lax.all_gather(both, axis, axis=dim, tiled=True), 0, [])
    for a, column in zip(arrays, columns):
        piece = filled[..., at : at + column.shape[along]]
        gathered.append(piece.reshape(*piece.shape[:along], *a.shape[along:]))
        at += column.shape[along]
    return tuple(gathered)


def split_up(value, dim, peers):
    before, after = (value.shape[:dim], value.shape[dim + 1 :])
    return jnp.moveaxis(value.reshape(*before, peers, -1, *after), dim, 0)


def summed_on_arrival(value, axis, dim):
    tiles = split_up(value, dim, lax.axis_size(axis))
    arrived = lax.all_to_all(tiles, axis, split_axis=0, concat_axis=0, tiled=True)
    return arrived.astype(jnp.float32).sum(axis=0)


def hadamard(order):
    places = jnp.arange(order, dtype=jnp.int32)
    common = places[:, None] & places[None, :]
    parity = jnp.zeros((order, order), jnp.int32)
    for bit_pos in range(order.bit_length() - 1):
        parity = parity ^ common >> bit_pos & 1
    return (1 - 2 * parity).astype(jnp.float32) / math.sqrt(order)


def rotate_blocks(values, sign_bits, width):
    signs = (2 * sign_bits - 1).astype(jnp.float32)
    blocks = (values * signs).reshape(values.shape[:-1] + (values.shape[-1] // width, width))
    turned = jnp.einsum("...bk,kj->...bj", blocks, hadamard(width))
    scales = (jnp.max(jnp.abs(turned), axis=-1) + 1e-06).astype(jnp.bfloat16)
    payload = (turned / scales.astype(jnp.float32)[..., None]).astype(jnp.bfloat16)
    return (payload, scales)


def rotary(vectors, positions):
    half_width = vectors.shape[-1] // 2
    frequency = jnp.exp(
        jnp.arange(half_width, dtype=jnp.float32) * (-2.0 * math.log(ROPE_BASE) / vectors.shape[-1])
    )
    angles = positions.astype(jnp.float32)[:, None] * frequency[None, :]
    cosine = jnp.cos(angles)[:, None, :]
    sines = jnp.sin(angles)[:, None, :]
    lower_half = vectors[..., :half_width]
    upper_half = vectors[..., half_width:]
    return jnp.concatenate(
        [lower_half * cosine - upper_half * sines, upper_half * cosine + lower_half * sines],
        axis=-1,
    )


def body(hidden, gain, sign_in, qkv_weight, out_weight, sign_attn, key_cache, value_cache, lengths):
    rows = hidden.astype(jnp.float32)
    squares = one_axis_at_a_time(jnp.sum(rows * rows, axis=1), WIDE)
    factor = lax.rsqrt(squares / D + 1e-05)
    normed = rows * factor[:, None] * gain.astype(jnp.float32)[None, :]
    payload, scales = rotate_blocks(normed, sign_in, HD)
    payload_all, scales_all = side_by_side((payload, scales), "narrow", 0, 2)
    weight_blocks = qkv_weight.reshape(payload.shape[1], HD, qkv_weight.shape[1])
    own_lists = key_cache.shape[0]
    products = jnp.einsum(
        "rbk,bkc->rbc", payload_all, weight_blocks, preferred_element_type=jnp.float32
    )
    projected = summed_on_arrival(
        jnp.einsum("rbc,rb->rc", products, scales_all.astype(jnp.float32)).astype(jnp.bfloat16),
        WIDE,
        0,
    )
    groups = key_cache.shape[1]
    grouped = projected.reshape(own_lists, groups, QG + 2, HD)
    queries = rotary(grouped[:, :, :QG, :].reshape(own_lists, groups * QG, HD), lengths)
    queries = queries.astype(jnp.bfloat16).reshape(own_lists, groups, QG, HD)
    keys_new = rotary(grouped[:, :, QG, :], lengths).astype(jnp.bfloat16)
    values_new = grouped[:, :, QG + 1, :].astype(jnp.bfloat16)
    inverse_root = 1.0 / math.sqrt(HD)
    live = jnp.arange(key_cache.shape[2], dtype=jnp.int32)[None, :] < lengths[:, None]
    live_mask = live[:, None, None, :]
    scores = (
        jnp.einsum("lgqk,lgsk->lgqs", queries, key_cache, preferred_element_type=jnp.float32)
        * inverse_root
    )
    fresh = (
        jnp.einsum("lgqk,lgk->lgq", queries, keys_new, preferred_element_type=jnp.float32)
        * inverse_root
    )
    scores = jnp.where(live_mask, scores, -1e30)
    peak = jnp.maximum(jnp.max(scores, axis=-1), fresh)
    weights = jnp.where(live_mask, jnp.exp(scores - peak[..., None]), 0.0)
    weight_new = jnp.exp(fresh - peak)
    denom_sum = jnp.sum(weights, axis=-1) + weight_new
    probs = (weights / denom_sum[..., None]).astype(jnp.bfloat16)
    prob_new = (weight_new / denom_sum).astype(jnp.bfloat16)
    attended = jnp.einsum("lgqs,lgsk->lgqk", probs, value_cache, preferred_element_type=jnp.float32)
    attended = (
        attended
        + prob_new.astype(jnp.float32)[..., None] * values_new.astype(jnp.float32)[:, :, None, :]
    )
    local_heads = groups * QG
    out_blocks, out_scale = rotate_blocks(
        attended.reshape(own_lists, local_heads * HD), sign_attn, HD
    )
    blocks_all, scale_all = side_by_side((out_blocks, out_scale), WIDE, 0, 2)
    head_weights = out_weight.reshape(local_heads, HD, out_weight.shape[1])
    products = jnp.einsum(
        "rhk,hkd->rhd", blocks_all, head_weights, preferred_element_type=jnp.float32
    )
    mixed = summed_on_arrival(
        jnp.einsum("rhd,rh->rd", products, scale_all.astype(jnp.float32)).astype(jnp.bfloat16),
        "narrow",
        0,
    )
    return (rows + mixed).astype(jnp.bfloat16)


def solution(mesh):
    split = Mesh(mesh.devices.reshape(4, 4, mesh.shape["narrow"]), ("wide_0", "wide_1", "narrow"))
    placed = (
        P("narrow", WIDE),
        P(WIDE),
        P(WIDE),
        P(WIDE, "narrow"),
        P("narrow", WIDE),
        P("narrow"),
        P(WIDE, "narrow", None, None),
        P(WIDE, "narrow", None, None),
        P(WIDE),
    )
    return jax.shard_map(
        body, mesh=split, in_specs=placed, out_specs=P("narrow", WIDE), check_vma=False
    )
```

profile of v0, /device:TPU:1, one launch (start us, length us, event | category | flops | bytes accessed | tf_op | source)
XLA Modules:
  0.0 118.0 jit_solution(16247789897836685528)
XLA Ops:
  0.0 0.7 add_convert_fusion.3
  0.7 0.7 convert_element_type.120
  1.4 0.9 fusion.37
  2.3 9.6 %psum.14 = f32[16]{0:T(128)S(1)} all-reduce(f32[16]{0:T(128)S(1)} %fusion.37), channel_id=1, replica_groups=mesh['wide_0'=4,'wide_1'=4,'narrow'=8] {'wide_0'}, use_global_device_ids=true, to_apply=%region_1.0 | all-reduce | flops 16 | bytes 128 | tf_op jit(solution)/shard_map/psum | solution.py:17
  11.8 9.7 %psum.15 = f32[16]{0:T(128)S(1)} all-reduce(f32[16]{0:T(128)S(1)} %psum.14), channel_id=1, replica_groups=mesh['wide_0'=4,'wide_1'=4,'narrow'=8] {'wide_1'}, use_global_device_ids=true, to_apply=%region_2.0 | all-reduce | flops 16 | bytes 128 | tf_op jit(solution)/shard_map/psum | solution.py:17
  21.5 0.8 fusion.40
  22.4 0.3 abs_reduce_fusion.1
  22.7 0.2 copy.28
  22.9 0.1 divide_convert_fusion.4
  23.0 18.0 %all_gather.6 = bf16[128,8,129]{2,1,0:T(8,128)(2,1)S(1)} all-gather(bf16[16,8,129]{2,1,0:T(8,128)(2,1)S(1)} %pad_maximum_fusion), channel_id=1, replica_groups=mesh['wide_0'=4,'wide_1'=4,'narrow'=8] {'narrow'}, dimensions={0}, use_global_device_ids=true | all-gather | bytes 297216 | tf_op jit(solution)/shard_map/all_gather | solution.py:24
  41.0 3.7 %convolution_bitcast_fusion = bf16[128,8,2304]{2,0,1:T(8,128)(2,1)S(1)} fusion(bf16[8,128,2304]{2,1,0:T(8,128)(2,1)} %bitcast.80, bf16[128,8,128]{2,1,0:T(8,128)(2,1)S(1)} %slice.45), kind=kOutput, calls=%fused_computation.8 | convolution fusion | flops 603979776 | bytes 9699328 | tf_op jit(solution)/shard_map/rbk,bkc->rbc/dot_general | solution.py:86
  44.8 3.4 %fusion = bf16[128,1,2304]{2,1,0:T(2,128)(2,1)S(1)} fusion(bf16[128,8,2304]{2,0,1:T(8,128)(2,1)S(1)} %convolution_bitcast_fusion, bf16[128,8,129]{2,1,0:T(8,128)(2,1)S(1)} %all_gather.6), kind=kOutput, calls=%fused_computation | convolution fusion | flops 4718592 | bytes 5570560 | tf_op jit(solution)/shard_map/rbc,rb->rc/dot_general | solution.py:90
  48.2 0.9 copy.68
  49.1 3.6 %all-to-all-start = ((bf16[16,8,2304]{2,1,0:T(8,128)(2,1)}), bf16[16,8,2304]{2,1,0:T(8,128)(2,1)S(1)}, u32[]{:S(2)}, u32[]{:S(2)}) async-start(bf16[16,8,2304]{2,1,0:T(8,128)(2,1)} %bitcast.77), calls=%async_computation | async-start | bytes 1179648 | tf_op jit(solution)/shard_map/all_to_all | solution.py:39
  52.7 0.1 iota_compare_fusion
  52.8 0.1 multiply_cosine_fusion.1
  52.9 10.8 %all-to-all-done = bf16[16,8,2304]{2,1,0:T(8,128)(2,1)S(1)} async-done(((bf16[16,8,2304]{2,1,0:T(8,128)(2,1)}), bf16[16,8,2304]{2,1,0:T(8,128)(2,1)S(1)}, u32[]{:S(2)}, u32[]{:S(2)}) %all-to-all-start) | async-done | bytes 589856 | tf_op jit(solution)/shard_map/all_to_all | solution.py:39
  63.9 0.1 fusion.63
  64.1 0.1 subtract_convert_fusion
  64.2 0.2 fusion.53
  64.4 5.8 %fusion.89 = (f32[8,16]{1,0:T(8,128)S(1)}, f32[8,16,4096]{2,1,0:T(8,128)S(1)}) fusion(bf16[8,1,4096,128]{3,2,1,0:T(8,128)(2,1)} %param.15, bf16[8,16,64]{2,1,0:T(8,128)(2,1)S(1)} %get-tuple-element.6, bf16[8,16,64]{2,1,0:T(8,128)(2,1)S(1)} %get-tuple-element.5, pred[8,4096]{1,0:T(8,128)(4,1)S(1)} %iota_compare_fusion), kind=kOutput, calls=%fused_computation.113 | convolution fusion | flops 135856000 | bytes 10551808 | tf_op jit(solution)/shard_map/lgqk,lgsk->lgqs/dot_general | solution.py:104
  70.2 0.6 fusion.14
  70.8 5.1 %abs_reduce_fusion = (f32[8,16]{1,0:T(8,128)S(1)}, f32[8,16,128]{2,1,0:T(8,128)S(1)}) fusion(bf16[8,1,4096,128]{3,2,1,0:T(8,128)(2,1)} %param.16, f32[8,16,4096]{2,1,0:T(8,128)S(1)} %get-tuple-element.20, f32[8,16]{1,0:T(8,128)S(1)} %get-tuple-element.8, f32[8,16]{1,0:T(8,128)S(1)} %multiply_maximum_fusion, pred[8,4096]{1,0:T(8,128)(4,1)S(1)} %iota_compare_fusion, ...), kind=kOutput, calls=%fused_computation.47 | convolution fusion | flops 141000576 | bytes 10598400 | tf_op jit(solution)/shard_map/...bk,kj->...bj/dot_general | solution.py:55
  75.9 0.1 copy.32
  76.1 0.1 divide_convert_fusion.3
  76.2 18.5 %all_gather.7 = bf16[128,16,129]{2,1,0:T(8,128)(2,1)S(1)} all-gather(bf16[8,16,129]{2,1,0:T(8,128)(2,1)S(1)} %pad_maximum_fusion.1), channel_id=1, replica_groups=mesh['wide_0'=4,'wide_1'=4,'narrow'=8] {'wide_0','wide_1'}, dimensions={0}, use_global_device_ids=true | all-gather | bytes 561408 | tf_op jit(solution)/shard_map/all_gather | solution.py:24
  94.7 0.1 slice.52
  94.8 3.4 %convolution_bitcast_fusion.1 = bf16[128,16,1024]{2,0,1:T(8,128)(2,1)S(1)} fusion(bf16[16,128,1024]{2,1,0:T(8,128)(2,1)} %bitcast.81, bf16[128,16,128]{2,1,0:T(8,128)(2,1)S(1)} %slice.52), kind=kOutput, calls=%fused_computation.11 | convolution fusion | flops 536870912 | bytes 8912896 | tf_op jit(solution)/shard_map/rhk,hkd->rhd/dot_general | solution.py:129
  98.3 2.6 %fusion.6 = bf16[128,1,1024]{2,1,0:T(2,128)(2,1)S(1)} fusion(bf16[128,16,1024]{2,0,1:T(8,128)(2,1)S(1)} %convolution_bitcast_fusion.1, bf16[128,16,129]{2,1,0:T(8,128)(2,1)S(1)} %all_gather.7), kind=kOutput, calls=%fused_computation.6 | convolution fusion | flops 4194304 | bytes 4980736 | tf_op jit(solution)/shard_map/rhd,rh->rd/dot_general | solution.py:133
  100.9 0.1 copy.69
  101.0 16.4 %all_to_all.10 = bf16[8,16,1024]{2,1,0:T(8,128)(2,1)S(1)} all-to-all(bf16[8,16,1024]{2,1,0:T(8,128)(2,1)S(1)} %bitcast.82), channel_id=1, replica_groups=mesh['wide_0'=4,'wide_1'=4,'narrow'=8] {'narrow'}, dimensions={0} | all-to-all | bytes 524288 | tf_op jit(solution)/shard_map/all_to_all | solution.py:39
  117.4 0.6 fusion.41
  (25 shorter events, 0.4 us)
Async XLA Ops:
  44.8 7.9 %copy-start.2 = (s32[8]{0:T(128)S(1)}, s32[8]{0:T(128)}, u32[]{:S(2)}) copy-start(s32[8]{0:T(128)} %param.17) | copy-start | bytes 100
  44.8 8.2 %copy-start.1 = (s32[2048]{0:T(1024)S(1)}, s32[2048]{0:T(1024)}, u32[]{:S(2)}) copy-start(s32[2048]{0:T(1024)} %param.14) | copy-start | bytes 24580
  49.1 14.7 %all-to-all-start = ((bf16[16,8,2304]{2,1,0:T(8,128)(2,1)}), bf16[16,8,2304]{2,1,0:T(8,128)(2,1)S(1)}, u32[]{:S(2)}, u32[]{:S(2)}) async-start(bf16[16,8,2304]{2,1,0:T(8,128)(2,1)} %bitcast.77), calls=%async_computation | async-start | bytes 1179648 | tf_op jit(solution)/shard_map/all_to_all | solution.py:39
  98.3 19.1 %copy-start = (bf16[16,1024]{1,0:T(8,128)(2,1)S(1)}, bf16[16,1024]{1,0:T(8,128)(2,1)}, u32[]{:S(2)}) copy-start(bf16[16,1024]{1,0:T(8,128)(2,1)} %param.9) | copy-start | bytes 98308
where the time goes:
time: 119 us; the launch traced here: 118 us
  blocking collectives  72.2 us (61%)
  matrix products  24.5 us (21%)
  waiting for transfers between devices  10.8 us (9%)
  other arithmetic  5.21 us (4%)
  starting transfers between devices  3.58 us (3%)
  local copies, waits for them, and re-layouts  1.44 us (1%)
    all_gather x2, blocking collectives, side_by_side(): lax.all_gather(both, axis, axis=dim, tiled=True)  36.5 us
    psum x2, blocking collectives, one_axis_at_a_time(): value = lax.psum(value, axis)  19.3 us
    all_to_all x1, blocking collectives, summed_on_arrival(): lax.all_to_all(tiles, axis, split_axis=0, concat_axis=0, tiled=True)  16.4 us
    all_to_all x1, waiting for transfers between devices, summed_on_arrival(): lax.all_to_all(tiles, axis, split_axis=0, concat_axis=0, tiled=True)  10.8 us
    dot_general x1, matrix products, body(): jnp.einsum('lgqk,lgsk->lgqs', queries, key_cache, preferred_element_type=...  5.79 us
    dot_general x2, matrix products, rotate_blocks(): turned = jnp.einsum('...bk,kj->...bj', blocks, hadamard(width))  5.36 us
    dot_general x1, matrix products, body(): jnp.einsum('rbk,bkc->rbc', payload_all, weight_blocks, preferred_element_...  3.71 us
    all_to_all x1, starting transfers between devices, summed_on_arrival(): lax.all_to_all(tiles, axis, split_axis=0, concat_axis=0, tiled=True)  3.58 us
  transfers between devices with their start and end apart: 1, of which 1 were waited for; matrix products, arithmetic and copies ran while one was open for 0% of the time, Pallas kernels for 0%

commit v1 on v0

--- a/solution.py
+++ b/solution.py
@@ -14,7 +14,7 @@
 
 def one_axis_at_a_time(value, axes):
     for axis in axes:
-        value = lax.psum(value, axis)
+        value = jnp.sum(lax.all_gather(value, axis), axis=0)
     return value
 
 

time: 119 us -> 123 us (1.034)
  local copies, waits for them, and re-layouts: 1.44 us -> 4.58 us
  between operations: 0.25 us -> 1.57 us
    psum x2 -> x0, blocking collectives: 19.3 us -> none  [one_axis_at_a_time(): value = lax.psum(value, axis)]
    unnamed x0 -> x2, blocking collectives: none -> 19.2 us
    unnamed x8 -> x14, local copies, waits for them, and re-layouts: 0.04 us -> 3.01 us
where the time goes in v1:
time: 123 us; the launch traced here: 122 us
  blocking collectives  72.2 us (59%)
  matrix products  24.5 us (20%)
  waiting for transfers between devices  10.8 us (9%)
  other arithmetic  5.26 us (4%)
  local copies, waits for them, and re-layouts  4.58 us (4%)
  starting transfers between devices  3.58 us (3%)
  between operations  1.57 us (1%)
    all_gather x2, blocking collectives, side_by_side(): lax.all_gather(both, axis, axis=dim, tiled=True)  36.5 us
    unnamed x2, blocking collectives  19.2 us
    all_to_all x1, blocking collectives, summed_on_arrival(): lax.all_to_all(tiles, axis, split_axis=0, concat_axis=0, tiled=True)  16.4 us
    all_to_all x1, waiting for transfers between devices, summed_on_arrival(): lax.all_to_all(tiles, axis, split_axis=0, concat_axis=0, tiled=True)  10.8 us
    dot_general x1, matrix products, body(): jnp.einsum('lgqk,lgsk->lgqs', queries, key_cache, preferred_element_type=...  5.79 us
    dot_general x2, matrix products, rotate_blocks(): turned = jnp.einsum('...bk,kj->...bj', blocks, hadamard(width))  5.36 us
    dot_general x1, matrix products, body(): jnp.einsum('rbk,bkc->rbc', payload_all, weight_blocks, preferred_element_...  3.71 us
    all_to_all x1, starting transfers between devices, summed_on_arrival(): lax.all_to_all(tiles, axis, split_axis=0, concat_axis=0, tiled=True)  3.58 us
  transfers between devices with their start and end apart: 1, of which 1 were waited for; matrix products, arithmetic and copies ran while one was open for 0% of the time, Pallas kernels for 0%

profile of v1, /device:TPU:1, one launch (start us, length us, event | category | flops | bytes accessed | tf_op | source)
XLA Modules:
  0.0 122.5 jit_solution(8889150019748252500)
XLA Ops:
  0.0 0.9 fusion.37
  0.9 1.2 %dynamic-slice = u32[1]{0:T(128)} dynamic-slice(u32[128]{0:T(128)} %constant.47, u32[]{:T(128)S(6)} %add.70), dynamic_slice_sizes={1} | dynamic-slice | bytes 12
  2.8 0.2 dynamic-update-slice
  3.0 9.5 %all-reduce = f32[64]{0:T(128)S(1)} all-reduce(f32[64]{0:T(128)S(1)} %dynamic-update-slice), channel_id=2, replica_groups=mesh['wide_0'=4,'wide_1'=4,'narrow'=8] {'wide_0'}, use_global_device_ids=true, to_apply=%add | all-reduce | flops 64 | bytes 512
  12.6 1.2 %dynamic-slice.1 = u32[1]{0:T(128)} dynamic-slice(u32[128]{0:T(128)} %constant.52, u32[]{:T(128)S(6)} %add.70), dynamic_slice_sizes={1} | dynamic-slice | bytes 12
  14.6 0.2 dynamic-update-slice.1
  14.8 9.7 %all-reduce.1 = f32[64]{0:T(128)S(1)} all-reduce(f32[64]{0:T(128)S(1)} %dynamic-update-slice.1), channel_id=3, replica_groups=mesh['wide_0'=4,'wide_1'=4,'narrow'=8] {'wide_1'}, use_global_device_ids=true, to_apply=%add.1 | all-reduce | flops 64 | bytes 512
  24.6 0.7 add_convert_fusion.3
  25.3 0.7 convert_element_type.120
  26.0 0.8 fusion.40
  26.9 0.3 abs_reduce_fusion.1
  27.2 0.2 copy.28
  27.5 18.0 %all_gather.22 = bf16[128,8,129]{2,1,0:T(8,128)(2,1)S(1)} all-gather(bf16[16,8,129]{2,1,0:T(8,128)(2,1)S(1)} %pad_maximum_fusion), channel_id=1, replica_groups=mesh['wide_0'=4,'wide_1'=4,'narrow'=8] {'narrow'}, dimensions={0}, use_global_device_ids=true | all-gather | bytes 297216 | tf_op jit(solution)/shard_map/all_gather | solution.py:24
  45.5 3.7 %convolution_bitcast_fusion = bf16[128,8,2304]{2,0,1:T(8,128)(2,1)S(1)} fusion(bf16[8,128,2304]{2,1,0:T(8,128)(2,1)} %bitcast.82, bf16[128,8,128]{2,1,0:T(8,128)(2,1)S(1)} %slice.45), kind=kOutput, calls=%fused_computation.8 | convolution fusion | flops 603979776 | bytes 9699328 | tf_op jit(solution)/shard_map/rbk,bkc->rbc/dot_general | solution.py:86
  49.2 3.4 %fusion = bf16[128,1,2304]{2,1,0:T(2,128)(2,1)S(1)} fusion(bf16[128,8,2304]{2,0,1:T(8,128)(2,1)S(1)} %convolution_bitcast_fusion, bf16[128,8,129]{2,1,0:T(8,128)(2,1)S(1)} %all_gather.22), kind=kOutput, calls=%fused_computation | convolution fusion | flops 4718592 | bytes 5570560 | tf_op jit(solution)/shard_map/rbc,rb->rc/dot_general | solution.py:90
  52.7 0.9 copy.68
  53.6 3.6 %all-to-all-start = ((bf16[16,8,2304]{2,1,0:T(8,128)(2,1)}), bf16[16,8,2304]{2,1,0:T(8,128)(2,1)S(1)}, u32[]{:S(2)}, u32[]{:S(2)}) async-start(bf16[16,8,2304]{2,1,0:T(8,128)(2,1)} %bitcast.79), calls=%async_computation | async-start | bytes 1179648 | tf_op jit(solution)/shard_map/all_to_all | solution.py:39
  57.3 0.1 multiply_cosine_fusion.1
  57.4 10.8 %all-to-all-done = bf16[16,8,2304]{2,1,0:T(8,128)(2,1)S(1)} async-done(((bf16[16,8,2304]{2,1,0:T(8,128)(2,1)}), bf16[16,8,2304]{2,1,0:T(8,128)(2,1)S(1)}, u32[]{:S(2)}, u32[]{:S(2)}) %all-to-all-start) | async-done | bytes 589856 | tf_op jit(solution)/shard_map/all_to_all | solution.py:39
  68.3 0.1 fusion.63
  68.6 0.2 fusion.53
  68.8 5.8 %fusion.89 = (f32[8,16]{1,0:T(8,128)S(1)}, f32[8,16,4096]{2,1,0:T(8,128)S(1)}) fusion(bf16[8,1,4096,128]{3,2,1,0:T(8,128)(2,1)} %param.15, bf16[8,16,64]{2,1,0:T(8,128)(2,1)S(1)} %get-tuple-element.6, bf16[8,16,64]{2,1,0:T(8,128)(2,1)S(1)} %get-tuple-element.5, pred[8,4096]{1,0:T(8,128)(4,1)S(1)} %iota_compare_fusion), kind=kOutput, calls=%fused_computation.113 | convolution fusion | flops 135856000 | bytes 10551808 | tf_op jit(solution)/shard_map/lgqk,lgsk->lgqs/dot_general | solution.py:104
  74.6 0.6 fusion.14
  75.3 5.1 %abs_reduce_fusion = (f32[8,16]{1,0:T(8,128)S(1)}, f32[8,16,128]{2,1,0:T(8,128)S(1)}) fusion(bf16[8,1,4096,128]{3,2,1,0:T(8,128)(2,1)} %param.16, f32[8,16,4096]{2,1,0:T(8,128)S(1)} %get-tuple-element.20, f32[8,16]{1,0:T(8,128)S(1)} %get-tuple-element.8, f32[8,16]{1,0:T(8,128)S(1)} %multiply_maximum_fusion, pred[8,4096]{1,0:T(8,128)(4,1)S(1)} %iota_compare_fusion, ...), kind=kOutput, calls=%fused_computation.47 | convolution fusion | flops 141000576 | bytes 10598400 | tf_op jit(solution)/shard_map/...bk,kj->...bj/dot_general | solution.py:55
  80.4 0.1 copy.32
  80.5 0.1 divide_convert_fusion.3
  80.7 18.5 %all_gather.23 = bf16[128,16,129]{2,1,0:T(8,128)(2,1)S(1)} all-gather(bf16[8,16,129]{2,1,0:T(8,128)(2,1)S(1)} %pad_maximum_fusion.1), channel_id=1, replica_groups=mesh['wide_0'=4,'wide_1'=4,'narrow'=8] {'wide_0','wide_1'}, dimensions={0}, use_global_device_ids=true | all-gather | bytes 561408 | tf_op jit(solution)/shard_map/all_gather | solution.py:24
  99.2 0.1 slice.52
  99.3 3.4 %convolution_bitcast_fusion.1 = bf16[128,16,1024]{2,0,1:T(8,128)(2,1)S(1)} fusion(bf16[16,128,1024]{2,1,0:T(8,128)(2,1)} %bitcast.83, bf16[128,16,128]{2,1,0:T(8,128)(2,1)S(1)} %slice.52), kind=kOutput, calls=%fused_computation.11 | convolution fusion | flops 536870912 | bytes 8912896 | tf_op jit(solution)/shard_map/rhk,hkd->rhd/dot_general | solution.py:129
  102.7 2.6 %fusion.6 = bf16[128,1,1024]{2,1,0:T(2,128)(2,1)S(1)} fusion(bf16[128,16,1024]{2,0,1:T(8,128)(2,1)S(1)} %convolution_bitcast_fusion.1, bf16[128,16,129]{2,1,0:T(8,128)(2,1)S(1)} %all_gather.23), kind=kOutput, calls=%fused_computation.6 | convolution fusion | flops 4194304 | bytes 4980736 | tf_op jit(solution)/shard_map/rhd,rh->rd/dot_general | solution.py:133
  105.4 16.4 %all_to_all.10 = bf16[8,16,1024]{2,1,0:T(8,128)(2,1)S(1)} all-to-all(bf16[8,16,1024]{2,1,0:T(8,128)(2,1)S(1)} %bitcast.84), channel_id=1, replica_groups=mesh['wide_0'=4,'wide_1'=4,'narrow'=8] {'narrow'}, dimensions={0} | all-to-all | bytes 524288 | tf_op jit(solution)/shard_map/all_to_all | solution.py:39
  121.8 0.6 fusion.41
  (35 shorter events, 0.9 us)
Async XLA Ops:
  49.2 7.9 %copy-start.2 = (s32[8]{0:T(128)S(1)}, s32[8]{0:T(128)}, u32[]{:S(2)}) copy-start(s32[8]{0:T(128)} %param.17) | copy-start | bytes 100
  49.2 8.2 %copy-start.1 = (s32[2048]{0:T(1024)S(1)}, s32[2048]{0:T(1024)}, u32[]{:S(2)}) copy-start(s32[2048]{0:T(1024)} %param.14) | copy-start | bytes 24580
  53.6 14.7 %all-to-all-start = ((bf16[16,8,2304]{2,1,0:T(8,128)(2,1)}), bf16[16,8,2304]{2,1,0:T(8,128)(2,1)S(1)}, u32[]{:S(2)}, u32[]{:S(2)}) async-start(bf16[16,8,2304]{2,1,0:T(8,128)(2,1)} %bitcast.79), calls=%async_computation | async-start | bytes 1179648 | tf_op jit(solution)/shard_map/all_to_all | solution.py:39
  102.7 19.1 %copy-start = (bf16[16,1024]{1,0:T(8,128)(2,1)S(1)}, bf16[16,1024]{1,0:T(8,128)(2,1)}, u32[]{:S(2)}) copy-start(bf16[16,1024]{1,0:T(8,128)(2,1)} %param.9) | copy-start | bytes 98308
